TPU v7x, 256 devices: a whole 4x4x8 slice. The times are simulated.
256 devices in a mesh: sect: 2 (over core), grp: 16 (over y_hi, z), tp: 8 (over y_lo, x).
Axes of the slice: x: 4, y: 4 (y_hi: 2, y_lo: 2; y = y_hi * 2 + y_lo), z: 8, core: 2. Of those that a mesh axis runs over, the one named last changes fastest.
Arguments:
- queries: bfloat16 [512, 128, 576], P('grp', ('sect', 'tp')), may hold values from -400 to 400, as said below
- latent_cache: bfloat16 [512, 128, 576], P('grp'), may hold values from -6 to 6, as said below
- cache_len: int32 [512], P('grp'), may hold values from 1 to 128, 32768 in all
- value_up: bfloat16 [128, 512, 128], P(('sect', 'tp')), may hold values from -0.25 to 0.25
- out_proj: bfloat16 [16384, 7168], P(('sect', 'tp'), 'grp'), may hold values from -0.046875 to 0.046875
- residual: bfloat16 [512, 7168], P(None, 'grp'), may hold values from -3 to 3
- w_gate: bfloat16 [16, 7168, 2048], P('grp', None, ('sect', 'tp')), may hold values from -0.0625 to 0.0625
- w_up: bfloat16 [16, 7168, 2048], P('grp', None, ('sect', 'tp')), may hold values from -0.0625 to 0.0625
- w_down: bfloat16 [16, 2048, 7168], P('grp', ('sect', 'tp')), may hold values from -0.1875 to 0.1875
- route_ids: int32 [512, 8], replicated, may hold values from 0 to 15, all different within a row; in each aligned block of 512 rows (0 to 511, 512 to 1023, ...) at most 384 rows name the same one
- route_weights: float32 [512, 8], replicated, may hold values from 0.1 to 0.6
Outputs:
- layer_out: bfloat16 [512, 7168], P(('sect', 'tp'), 'grp')
Inputs may be any that keep to these rules, and one draw needn't show every extreme that they name: `queries`: every entry lies in this range. `latent_cache`: every entry lies in this range. `route_ids`: each row names 8 different experts; every expert is named by at most 384 rows, and one expert by exactly 384. `cache_len`: some row has exactly 128 filled positions.
All inputs are finite; a program needn't handle non-finite values. No bound on the sum of `cache_len` on one device may be relied on, other than what follows from the above.
Results may differ from a plain program's by a relative error of at most 0.018.
Values may be sent and summed in bfloat16 or wider, within the bound.
A program may use at most 128 MiB of HBM per device.

v0:
```python
import jax
import jax.numpy as jnp
from jax import lax
from jax.sharding import PartitionSpec as P

LAT = 512
VDIM = 128
TOP = 8
SOFTMAX_SCALE = 0.0721688
MASK_VALUE = -1e30


def slot_tables(route_ids, route_weights, expert_count, capacity):
    row_total = route_ids.shape[0]
    expert_ids = jnp.arange(expert_count, dtype=jnp.int32)
    matches = route_ids[None, :, :] == expert_ids[:, None, None]
    chosen = jnp.any(matches, axis=2)
    weight = jnp.sum(jnp.where(matches, route_weights[None, :, :], 0.0), axis=2)
    slot_rank = jnp.cumsum(chosen.astype(jnp.int32), axis=1) - 1
    slot_ids = jnp.arange(capacity, dtype=jnp.int32)
    placed = chosen[:, :, None] & (slot_rank[:, :, None] == slot_ids[None, None, :])
    row_ids = jnp.arange(row_total, dtype=jnp.int32)
    slot_rows = jnp.sum(jnp.where(placed, row_ids[None, :, None], 0), axis=1)
    slot_valid = jnp.any(placed, axis=1)
    slot_weight = jnp.sum(jnp.where(placed, weight[:, :, None], 0.0), axis=1)
    return (placed, slot_rows, slot_valid, slot_weight)


def pick_slots(source_rows, slot_rows, slot_valid):
    picked = jnp.take(source_rows, slot_rows, axis=0)
    return jnp.where(slot_valid[:, :, None], picked, jnp.zeros_like(picked))


def on_device(
    queries,
    latent_cache,
    cache_len,
    value_up,
    out_proj,
    residual,
    w_gate,
    w_up,
    w_down,
    route_ids,
    route_weights,
):
    local_rows = queries.shape[0]
    local_heads = queries.shape[1]
    scores = (
        jnp.einsum("rhk,rlk->rhl", queries, latent_cache, preferred_element_type=jnp.float32)
        * SOFTMAX_SCALE
    )
    positions = jnp.arange(latent_cache.shape[1], dtype=jnp.int32)
    in_range = positions[None, None, :] < cache_len[:, None, None]
    masked = jnp.where(in_range, scores, MASK_VALUE)
    row_max = jnp.max(masked, axis=2, keepdims=True)
    exp_scores = jnp.where(in_range, jnp.exp(masked - row_max), 0.0)
    probs = (exp_scores / jnp.sum(exp_scores, axis=2, keepdims=True)).astype(jnp.bfloat16)
    latent_out = jnp.einsum(
        "rhl,rlc->rhc", probs, latent_cache[:, :, :LAT], preferred_element_type=jnp.float32
    ).astype(jnp.bfloat16)
    heads_out = jnp.einsum("rhc,hcv->rhv", latent_out, value_up, preferred_element_type=jnp.float32)
    heads_out = heads_out.astype(jnp.bfloat16).reshape(local_rows, local_heads * VDIM)
    partial_attn = jnp.dot(
        lax.all_gather(heads_out, "grp", axis=0, tiled=True),
        out_proj,
        preferred_element_type=jnp.float32,
    )
    row_total = residual.shape[0]
    expert_count = lax.axis_size("grp")
    tensor_count = lax.axis_size(("sect", "tp"))
    tensor_index = lax.axis_index(("sect", "tp"))
    own_expert = lax.axis_index("grp")
    capacity = min(row_total, row_total * TOP * 3 // (2 * expert_count))
    placed, slot_rows, slot_valid, slot_weight = slot_tables(
        route_ids, route_weights, expert_count, capacity
    )
    share_rows = row_total // tensor_count
    attention = lax.psum(partial_attn, ("sect", "tp"))
    layer_input = (residual.astype(jnp.float32) + attention).astype(jnp.bfloat16)
    own_rows = lax.dynamic_slice_in_dim(layer_input, tensor_index * share_rows, share_rows, 0)
    outgoing = pick_slots(layer_input, slot_rows, slot_valid)
    received = lax.all_to_all(outgoing, "grp", split_axis=0, concat_axis=2, tiled=True)
    expert_in = received[0]
    own_weight = lax.dynamic_index_in_dim(slot_weight, own_expert, 0, keepdims=False)
    gate_value = jnp.dot(expert_in, w_gate[0], preferred_element_type=jnp.float32)
    up_value = jnp.dot(expert_in, w_up[0], preferred_element_type=jnp.float32)
    hidden = (own_weight[:, None] * jax.nn.silu(gate_value) * up_value).astype(jnp.bfloat16)
    own_placed = lax.dynamic_index_in_dim(placed, own_expert, 0, keepdims=False).astype(
        jnp.bfloat16
    )
    hidden_rows = jnp.dot(own_placed, hidden, preferred_element_type=jnp.float32).astype(
        jnp.bfloat16
    )
    expert_term = jnp.dot(hidden_rows, w_down[0], preferred_element_type=jnp.float32)
    column_sums = lax.psum_scatter(
        expert_term.astype(jnp.bfloat16), "grp", scatter_dimension=1, tiled=True
    )
    routed_sum = lax.psum_scatter(
        column_sums, ("sect", "tp"), scatter_dimension=0, tiled=True
    ).astype(jnp.float32)
    return (own_rows.astype(jnp.float32) + routed_sum).astype(jnp.bfloat16)


def solution(mesh):
    return jax.shard_map(
        on_device,
        mesh=mesh,
        in_specs=(
            P("grp", ("sect", "tp"), None),
            P("grp", None, None),
            P("grp"),
            P(("sect", "tp"), None, None),
            P(("sect", "tp"), "grp"),
            P(None, "grp"),
            P("grp", None, ("sect", "tp")),
            P("grp", None, ("sect", "tp")),
            P("grp", ("sect", "tp"), None),
            P(),
            P(),
        ),
        out_specs=P(("sect", "tp"), "grp"),
        check_vma=False,
    )
```

profile of v0, /device:TPU:24, one launch (start us, length us, event | category | flops | bytes accessed | tf_op | source)
XLA Modules:
  0.0 729.3 jit_solution(1491521176456997909)
XLA Ops:
  6.5 0.0 copy-start
  6.5 0.0 all-gather.2.cloned.1.call-start
  6.5 0.9 iota_compare_fusion.2
  7.4 0.0 copy-start.1
  7.4 0.0 copy-start.3
  7.4 3.5 fusion.33
  10.9 0.0 copy-start.2
  10.9 3.5 fusion.9
  14.3 0.0 copy-done.1
  14.3 0.4 fusion.22
  14.7 0.6 copy.63
  15.3 0.0 all-gather.2.cloned.1.call-update
  15.4 0.0 all-reduce.2.cloned.1.call-start
  15.4 0.0 copy-done.3
  15.4 0.1 fusion.28
  15.5 1.2 reduce-window.6
  16.7 0.2 slice_reduce_fusion
  16.9 0.1 copy_bitcast_fusion.1
  17.0 3.3 select_reduce_fusion
  20.4 75.0 %all-gather.2.cloned.1.call-done = bf16[512,1024]{1,0:T(8,128)(2,1)} async-done(((bf16[32,1024]{1,0:T(8,128)(2,1)}), bf16[512,1024]{1,0:T(8,128)(2,1)}) %all-gather.2.cloned.1.call-update) | async-done | bytes 1048592 | tf_op jit(solution)/shard_map/all_gather | solution.py:65
  95.4 3.2 fusion.34
  98.6 0.0 all-reduce.2.cloned.1.call-update
  98.6 0.0 copy-done.2
  98.6 0.2 copy.42
  98.8 5.1 fusion.1
  104.0 131.3 %all-reduce.2.cloned.1.call-done = f32[512,448]{1,0:T(8,128)} async-done(((f32[512,448]{1,0:T(8,128)}), f32[512,448]{1,0:T(8,128)}) %all-reduce.2.cloned.1.call-update) | async-done | bytes 917520 | tf_op jit(solution)/shard_map/psum | solution.py:79
  235.3 1.4 add_convert_fusion
  236.7 25.4 %gather_fusion = bf16[6144,448]{1,0:T(8,128)(2,1)} fusion(bf16[512,448]{1,0:T(8,128)(2,1)S(1)} %add_convert_fusion, s32[6144]{0:T(1024)S(1)} %broadcast_clamp_fusion), kind=kCustom, calls=%fused_computation | custom fusion | bytes 11034624 | tf_op jit(solution)/shard_map/jit(_take)/gather | solution.py:30
  262.1 8.3 %copy.49 = bf16[16,384,448]{1,2,0:T(8,128)(2,1)} copy(bf16[16,384,448]{2,1,0:T(8,128)(2,1)} %bitcast.52) | data formatting | bytes 11010048 | tf_op jit(solution)/shard_map/jit(_take)/gather | solution.py:30
  270.5 5.9 select_select_fusion
  276.3 0.0 copy-start.4
  276.3 10.1 %all-to-all-start = ((bf16[16,384,448]{1,2,0:T(8,128)(2,1)}), bf16[16,384,448]{1,2,0:T(8,128)(2,1)}, u32[]{:S(2)}, u32[]{:S(2)}) async-start(bf16[16,384,448]{1,2,0:T(8,128)(2,1)} %select_select_fusion), calls=%async_computation | async-start | bytes 11010048 | tf_op jit(solution)/shard_map/all_to_all | solution.py:83
  286.5 0.0 reduce-scatter.5.cloned.1.call-start
  286.5 0.0 copy-done.4
  286.5 0.1 select_reduce_fusion.2
  286.6 4.6 select_reduce_fusion.1
  291.2 113.3 %all-to-all-done = bf16[16,384,448]{1,2,0:T(8,128)(2,1)} async-done(((bf16[16,384,448]{1,2,0:T(8,128)(2,1)}), bf16[16,384,448]{1,2,0:T(8,128)(2,1)}, u32[]{:S(2)}, u32[]{:S(2)}) %all-to-all-start) | async-done | bytes 5505056 | tf_op jit(solution)/shard_map/all_to_all | solution.py:83
  404.6 0.0 copy-start.5
  404.6 4.9 fusion.7
  409.4 0.0 copy-done.5
  409.4 4.2 fusion.16
  413.7 0.0 copy-done
  413.7 5.4 convolution_convert_fusion
  419.1 0.0 reduce-scatter.5.cloned.1.call-update
  419.2 0.0 reduce-scatter.7.cloned.1.call-start
  419.2 230.0 %reduce-scatter.5.cloned.1.call-done = bf16[512,448]{0,1:T(8,128)(2,1)} async-done(((bf16[512,7168]{0,1:T(8,128)(2,1)}), bf16[512,448]{0,1:T(8,128)(2,1)}) %reduce-scatter.5.cloned.1.call-update) | async-done | bytes 458768 | tf_op jit(solution)/shard_map/reduce_scatter | solution.py:96
  649.3 2.0 copy.52
  651.3 0.0 reduce-scatter.7.cloned.1.call-update
  651.3 70.1 %reduce-scatter.7.cloned.1.call-done = bf16[32,448]{1,0:T(8,128)(2,1)} async-done(((bf16[512,448]{1,0:T(8,128)(2,1)}), bf16[32,448]{1,0:T(8,128)(2,1)}) %reduce-scatter.7.cloned.1.call-update) | async-done | bytes 28688 | tf_op jit(solution)/shard_map/reduce_scatter | solution.py:99
  721.4 1.4 add_convert_fusion.1
  (8 shorter events, 0.1 us)
Async XLA Ops:
  6.5 407.1 %copy-start = (bf16[1,128,7168]{2,1,0:T(8,128)(2,1)S(1)}, bf16[1,128,7168]{2,1,0:T(8,128)(2,1)}, u32[]{:S(2)}) copy-start(bf16[1,128,7168]{2,1,0:T(8,128)(2,1)} %param.19) | copy-start | bytes 5505028
  6.5 88.8 %all-gather.2.cloned.1.call-start = ((), (), s32[]{:S(2)}) async-start(), calls=%async_computation.3 | async-start | bytes 1114112 | tf_op jit(solution)/shard_map/all_gather | solution.py:65
  7.4 6.9 copy-start.1
  7.4 8.0 %copy-start.3 = (s32[512,8]{0,1:T(8,128)S(1)}, s32[512,8]{0,1:T(8,128)}, u32[]{:S(2)}) copy-start(s32[512,8]{0,1:T(8,128)} %param.20) | copy-start | bytes 49156
  10.9 87.7 %copy-start.2 = (bf16[512,448]{0,1:T(8,128)(2,1)S(1)}, bf16[512,448]{0,1:T(8,128)(2,1)}, u32[]{:S(2)}) copy-start(bf16[512,448]{0,1:T(8,128)(2,1)} %param.16) | copy-start | bytes 1376260
  15.4 220.0 %all-reduce.2.cloned.1.call-start = ((), (), s32[]{:S(2)}) async-start(), calls=%async_computation.4 | async-start | bytes 2097152 | tf_op jit(solution)/shard_map/psum | solution.py:79
  276.3 10.2 %copy-start.4 = (f32[512,8]{0,1:T(8,128)S(1)}, f32[512,8]{0,1:T(8,128)}, u32[]{:S(2)}) copy-start(f32[512,8]{0,1:T(8,128)} %param.21) | copy-start | bytes 49156
  276.3 128.2 %all-to-all-start = ((bf16[16,384,448]{1,2,0:T(8,128)(2,1)}), bf16[16,384,448]{1,2,0:T(8,128)(2,1)}, u32[]{:S(2)}, u32[]{:S(2)}) async-start(bf16[16,384,448]{1,2,0:T(8,128)(2,1)} %select_select_fusion), calls=%async_computation | async-start | bytes 11010048 | tf_op jit(solution)/shard_map/all_to_all | solution.py:83
  286.5 362.8 %reduce-scatter.5.cloned.1.call-start = ((), (), s32[]{:S(2)}) async-start(), calls=%async_computation.5 | async-start | bytes 7798784 | tf_op jit(solution)/shard_map/reduce_scatter | solution.py:96
  404.6 4.9 copy-start.5
  419.2 302.3 %reduce-scatter.7.cloned.1.call-start = ((), (), s32[]{:S(2)}) async-start(), calls=%async_computation.6 | async-start | bytes 557056 | tf_op jit(solution)/shard_map/reduce_scatter | solution.py:99
Sparse Core Ops, SparseCore 0:
  15.5 79.8 all-gather.1
  98.7 136.5 all-reduce.1
  419.3 229.9 reduce-scatter.4
  651.6 69.7 reduce-scatter.6
where the time goes:
time: 730 us; the launch traced here: 729 us
  waiting for transfers between devices  620 us (85%)
  local copies, waits for them, and re-layouts  36.9 us (5%)
  matrix products  25 us (3%)
  other arithmetic  24 us (3%)
  between operations  13.3 us (2%)
  starting transfers between devices  10.2 us (1%)
    reduce_scatter x1, waiting for transfers between devices, on_device(): lax.psum_scatter(expert_term.astype(jnp.bfloat16), 'grp', scatter_dimensi...  230 us
    psum x1, waiting for transfers between devices, on_device(): attention = lax.psum(partial_attn, ('sect', 'tp'))  131 us
    all_to_all x1, waiting for transfers between devices, on_device(): lax.all_to_all(outgoing, 'grp', split_axis=0, concat_axis=2, tiled=True)  113 us
    all_gather x1, waiting for transfers between devices, on_device(): lax.all_gather(heads_out, 'grp', axis=0, tiled=True)  75 us
    reduce_scatter x1, waiting for transfers between devices, on_device(): lax.psum_scatter(column_sums, ('sect', 'tp'), scatter_dimension=0, tiled=...  70.1 us
    gather x2, local copies, waits for them, and re-layouts, pick_slots(): picked = jnp.take(source_rows, slot_rows, axis=0)  33.8 us
  transfers between devices with their start and end apart: 5, of which 5 were waited for; matrix products, arithmetic and copies ran while one was open for 2% of the time, Pallas kernels for 0%

commit v1 on v0

--- a/solution.py
+++ b/solution.py
@@ -8,6 +8,13 @@
 TOP = 8
 SOFTMAX_SCALE = 0.0721688
 MASK_VALUE = -1e30
+
+
+def exchange_gather(x, mesh_axis, dim):
+    size = lax.axis_size(mesh_axis)
+    shards = jnp.stack([x for _ in range(size)])
+    shards = lax.all_to_all(shards, mesh_axis, split_axis=0, concat_axis=0)
+    return jnp.concatenate(shards, axis=dim)
 
 
 def slot_tables(route_ids, route_weights, expert_count, capacity):
@@ -62,9 +69,7 @@
     heads_out = jnp.einsum("rhc,hcv->rhv", latent_out, value_up, preferred_element_type=jnp.float32)
     heads_out = heads_out.astype(jnp.bfloat16).reshape(local_rows, local_heads * VDIM)
     partial_attn = jnp.dot(
-        lax.all_gather(heads_out, "grp", axis=0, tiled=True),
-        out_proj,
-        preferred_element_type=jnp.float32,
+        exchange_gather(heads_out, "grp", 0), out_proj, preferred_element_type=jnp.float32
     )
     row_total = residual.shape[0]
     expert_count = lax.axis_size("grp")

time: 730 us -> 688 us (0.942)
  waiting for transfers between devices: 620 us -> 566 us
  starting transfers between devices: 10.2 us -> 21.7 us
    all_gather x1 -> x0, waiting for transfers between devices: 75 us -> none  [on_device(): lax.all_gather(heads_out, 'grp', axis=0, tiled=True)]
    all_to_all x0 -> x1, waiting for transfers between devices: none -> 20.8 us  [exchange_gather(): shards = lax.all_to_all(shards, mesh_axis, split_axis=0, concat_axis=0)]
    all_to_all x0 -> x1, starting transfers between devices: none -> 11.4 us  [exchange_gather(): shards = lax.all_to_all(shards, mesh_axis, split_axis=0, concat_axis=0)]
where the time goes in v1:
time: 688 us; the launch traced here: 687 us
  waiting for transfers between devices  566 us (82%)
  local copies, waits for them, and re-layouts  37.4 us (5%)
  matrix products  24.7 us (4%)
  other arithmetic  24 us (3%)
  starting transfers between devices  21.7 us (3%)
  between operations  13.3 us (2%)
    reduce_scatter x1, waiting for transfers between devices, on_device(): lax.psum_scatter(expert_term.astype(jnp.bfloat16), 'grp', scatter_dimensi...  230 us
    psum x1, waiting for transfers between devices, on_device(): attention = lax.psum(partial_attn, ('sect', 'tp'))  132 us
    all_to_all x1, waiting for transfers between devices, on_device(): lax.all_to_all(outgoing, 'grp', split_axis=0, concat_axis=2, tiled=True)  113 us
    reduce_scatter x1, waiting for transfers between devices, on_device(): lax.psum_scatter(column_sums, ('sect', 'tp'), scatter_dimension=0, tiled=...  70.4 us
    gather x2, local copies, waits for them, and re-layouts, pick_slots(): picked = jnp.take(source_rows, slot_rows, axis=0)  33.8 us
    all_to_all x1, waiting for transfers between devices, exchange_gather(): shards = lax.all_to_all(shards, mesh_axis, split_axis=0, concat_axis=0)  20.8 us
  transfers between devices with their start and end apart: 5, of which 5 were waited for; matrix products, arithmetic and copies ran while one was open for 2% of the time, Pallas kernels for 0%

profile of v1, /device:TPU:24, one launch (start us, length us, event | category | flops | bytes accessed | tf_op | source)
XLA Modules:
  0.0 687.1 jit_solution(14217199787866913405)
XLA Ops:
  6.5 0.0 copy-start
  6.5 0.9 iota_compare_fusion.2
  7.4 0.0 copy-start.1
  7.4 3.5 fusion.33
  10.9 0.0 copy-start.3
  10.9 3.4 fusion.9
  14.3 0.0 copy-done.1
  14.3 0.0 copy-start.2
  14.3 0.4 fusion.22
  14.7 1.1 stack.3
  15.8 11.4 %all-to-all-start = ((bf16[16,32,1024]{2,1,0:T(8,128)(2,1)}), bf16[16,32,1024]{2,1,0:T(8,128)(2,1)S(1)}, u32[]{:S(2)}, u32[]{:S(2)}) async-start(bf16[16,32,1024]{2,1,0:T(8,128)(2,1)} %stack.3), calls=%async_computation | async-start | bytes 2097152 | tf_op jit(solution)/shard_map/all_to_all | solution.py:16
  27.2 0.0 all-reduce.2.cloned.1.call-start
  27.3 0.0 copy-done.3
  27.3 0.1 fusion.28
  27.4 1.2 reduce-window.6
  28.6 0.2 slice_reduce_fusion
  28.8 0.1 copy_bitcast_fusion.1
  28.9 3.3 select_reduce_fusion
  32.3 20.8 %all-to-all-done = bf16[16,32,1024]{2,1,0:T(8,128)(2,1)S(1)} async-done(((bf16[16,32,1024]{2,1,0:T(8,128)(2,1)}), bf16[16,32,1024]{2,1,0:T(8,128)(2,1)S(1)}, u32[]{:S(2)}, u32[]{:S(2)}) %all-to-all-start) | async-done | bytes 1048608 | tf_op jit(solution)/shard_map/all_to_all | solution.py:16
  53.0 2.9 fusion.34
  56.0 0.0 all-reduce.2.cloned.1.call-update
  56.0 0.0 copy-done.2
  56.0 0.2 copy.42
  56.3 5.1 fusion.1
  61.4 131.6 %all-reduce.2.cloned.1.call-done = f32[512,448]{1,0:T(8,128)} async-done(((f32[512,448]{1,0:T(8,128)}), f32[512,448]{1,0:T(8,128)}) %all-reduce.2.cloned.1.call-update) | async-done | bytes 917520 | tf_op jit(solution)/shard_map/psum | solution.py:84
  193.0 1.4 add_convert_fusion
  194.4 25.4 %gather_fusion = bf16[6144,448]{1,0:T(8,128)(2,1)} fusion(bf16[512,448]{1,0:T(8,128)(2,1)S(1)} %add_convert_fusion, s32[6144]{0:T(1024)S(1)} %broadcast_clamp_fusion), kind=kCustom, calls=%fused_computation | custom fusion | bytes 11034624 | tf_op jit(solution)/shard_map/jit(_take)/gather | solution.py:37
  219.8 8.3 %copy.49 = bf16[16,384,448]{1,2,0:T(8,128)(2,1)} copy(bf16[16,384,448]{2,1,0:T(8,128)(2,1)} %bitcast.53) | data formatting | bytes 11010048 | tf_op jit(solution)/shard_map/jit(_take)/gather | solution.py:37
  228.2 5.9 select_select_fusion
  234.0 0.0 copy-start.4
  234.0 10.1 %all-to-all-start.1 = ((bf16[16,384,448]{1,2,0:T(8,128)(2,1)}), bf16[16,384,448]{1,2,0:T(8,128)(2,1)}, u32[]{:S(2)}, u32[]{:S(2)}) async-start(bf16[16,384,448]{1,2,0:T(8,128)(2,1)} %select_select_fusion), calls=%async_computation.1 | async-start | bytes 11010048 | tf_op jit(solution)/shard_map/all_to_all | solution.py:88
  244.1 0.0 reduce-scatter.5.cloned.1.call-start
  244.2 0.0 copy-done.4
  244.2 0.1 select_reduce_fusion.2
  244.3 4.6 select_reduce_fusion.1
  248.9 113.3 %all-to-all-done.1 = bf16[16,384,448]{1,2,0:T(8,128)(2,1)} async-done(((bf16[16,384,448]{1,2,0:T(8,128)(2,1)}), bf16[16,384,448]{1,2,0:T(8,128)(2,1)}, u32[]{:S(2)}, u32[]{:S(2)}) %all-to-all-start.1) | async-done | bytes 5505056 | tf_op jit(solution)/shard_map/all_to_all | solution.py:88
  362.2 0.0 copy-start.5
  362.2 4.9 fusion.7
  367.1 0.0 copy-done.5
  367.1 4.2 fusion.16
  371.4 0.0 copy-done
  371.4 5.5 convolution_convert_fusion
  376.8 0.0 reduce-scatter.5.cloned.1.call-update
  376.8 0.0 reduce-scatter.7.cloned.1.call-start
  376.9 229.9 %reduce-scatter.5.cloned.1.call-done = bf16[512,448]{0,1:T(8,128)(2,1)} async-done(((bf16[512,7168]{0,1:T(8,128)(2,1)}), bf16[512,448]{0,1:T(8,128)(2,1)}) %reduce-scatter.5.cloned.1.call-update) | async-done | bytes 458768 | tf_op jit(solution)/shard_map/reduce_scatter | solution.py:101
  606.8 2.0 copy.52
  608.8 0.0 reduce-scatter.7.cloned.1.call-update
  608.8 70.4 %reduce-scatter.7.cloned.1.call-done = bf16[32,448]{1,0:T(8,128)(2,1)} async-done(((bf16[512,448]{1,0:T(8,128)(2,1)}), bf16[32,448]{1,0:T(8,128)(2,1)}) %reduce-scatter.7.cloned.1.call-update) | async-done | bytes 28688 | tf_op jit(solution)/shard_map/reduce_scatter | solution.py:104
  679.2 1.4 add_convert_fusion.1
  (9 shorter events, 0.1 us)
Async XLA Ops:
  6.5 364.8 %copy-start = (bf16[1,128,7168]{2,1,0:T(8,128)(2,1)S(1)}, bf16[1,128,7168]{2,1,0:T(8,128)(2,1)}, u32[]{:S(2)}) copy-start(bf16[1,128,7168]{2,1,0:T(8,128)(2,1)} %param.19) | copy-start | bytes 5505028
  7.4 6.9 %copy-start.1 = (bf16[8,512,128]{2,1,0:T(8,128)(2,1)S(1)}, bf16[8,512,128]{2,1,0:T(8,128)(2,1)}, u32[]{:S(2)}) copy-start(bf16[8,512,128]{2,1,0:T(8,128)(2,1)} %param.14) | copy-start | bytes 3145732
  10.9 16.4 %copy-start.3 = (s32[512,8]{0,1:T(8,128)S(1)}, s32[512,8]{0,1:T(8,128)}, u32[]{:S(2)}) copy-start(s32[512,8]{0,1:T(8,128)} %param.20) | copy-start | bytes 49156
  14.3 41.7 %copy-start.2 = (bf16[512,448]{0,1:T(8,128)(2,1)S(1)}, bf16[512,448]{0,1:T(8,128)(2,1)}, u32[]{:S(2)}) copy-start(bf16[512,448]{0,1:T(8,128)(2,1)} %param.16) | copy-start | bytes 1376260
  15.8 37.2 %all-to-all-start = ((bf16[16,32,1024]{2,1,0:T(8,128)(2,1)}), bf16[16,32,1024]{2,1,0:T(8,128)(2,1)S(1)}, u32[]{:S(2)}, u32[]{:S(2)}) async-start(bf16[16,32,1024]{2,1,0:T(8,128)(2,1)} %stack.3), calls=%async_computation | async-start | bytes 2097152 | tf_op jit(solution)/shard_map/all_to_all | solution.py:16
  27.2 165.7 %all-reduce.2.cloned.1.call-start = ((), (), s32[]{:S(2)}) async-start(), calls=%async_computation.4 | async-start | bytes 2097152 | tf_op jit(solution)/shard_map/psum | solution.py:84
  234.0 10.2 %copy-start.4 = (f32[512,8]{0,1:T(8,128)S(1)}, f32[512,8]{0,1:T(8,128)}, u32[]{:S(2)}) copy-start(f32[512,8]{0,1:T(8,128)} %param.21) | copy-start | bytes 49156
  234.0 128.2 %all-to-all-start.1 = ((bf16[16,384,448]{1,2,0:T(8,128)(2,1)}), bf16[16,384,448]{1,2,0:T(8,128)(2,1)}, u32[]{:S(2)}, u32[]{:S(2)}) async-start(bf16[16,384,448]{1,2,0:T(8,128)(2,1)} %select_select_fusion), calls=%async_computation.1 | async-start | bytes 11010048 | tf_op jit(solution)/shard_map/all_to_all | solution.py:88
  244.1 362.6 %reduce-scatter.5.cloned.1.call-start = ((), (), s32[]{:S(2)}) async-start(), calls=%async_computation.5 | async-start | bytes 7798784 | tf_op jit(solution)/shard_map/reduce_scatter | solution.py:101
  362.2 4.9 copy-start.5
  376.8 302.4 %reduce-scatter.7.cloned.1.call-start = ((), (), s32[]{:S(2)}) async-start(), calls=%async_computation.6 | async-start | bytes 557056 | tf_op jit(solution)/shard_map/reduce_scatter | solution.py:104
Sparse Core Ops, SparseCore 0:
  56.1 136.8 all-reduce.1
  377.0 229.7 reduce-scatter.4
  609.3 69.8 reduce-scatter.6
